TPU v7x, 256 devices: a whole 4x4x8 slice. The times are simulated.
256 devices in a mesh: ctx: 16 (over x, y), head: 16 (over z, core).
Axes of the slice: x: 4, y: 4, z: 8, core: 2. Of those that a mesh axis runs over, the one named last changes fastest.
Arguments:
- tokens: bfloat16 [8192, 8192], P('ctx'), may hold values from -6 to 6
- w_zx: bfloat16 [8192, 2, 8192], P('ctx', None, 'head'), may hold values from -0.0625 to 0.0625
- zx_scale: float32 [2, 8192], P(None, 'head'), may hold values from 0.5 to 2
- w_bc: bfloat16 [8192, 8, 512], P('ctx'), may hold values from -0.0625 to 0.0625
- bc_scale: float32 [8, 512], replicated, may hold values from 0.5 to 2
- w_dt: bfloat16 [8192, 128], P('ctx', 'head'), may hold values from -0.0625 to 0.0625
- conv_x: float32 [5, 8192], P(None, 'head'), may hold values from -3 to 3
- conv_bc: float32 [5, 8, 512], replicated, may hold values from -3 to 3
- tail_x: bfloat16 [3, 8192], P(None, 'head'), may hold values from -6 to 6
- tail_bc: bfloat16 [3, 8, 512], replicated, may hold values from -6 to 6
- head_params: float32 [3, 128], P(None, 'head'), may hold values from -12 to 2, as said below
- init_state: float32 [128, 64, 256], P('head'), may hold values from -1.5 to 1.5
- norm_gain: float32 [8192], P('head'), may hold values from 0.5 to 1.5
Outputs:
- mixed: bfloat16 [8192, 8192], P('ctx', 'head')
Inputs may be any that keep to these rules, and one draw needn't show every extreme that they name: `head_params`: row 0 lies in -3.5 to -2.5 and row 2 in 0.5 to 1.5.
All inputs are finite; a program needn't handle non-finite values.
Results may differ from a plain program's by a relative error of at most 0.0052.
Values may be sent and summed in bfloat16 or wider, within the bound.
A program may use at most 256 MiB of HBM per device.

v0:
```python
import jax
import jax.numpy as jnp
from jax import lax
from jax.sharding import PartitionSpec as P

H = 128
P_SIZE = 64
N = 256
G = 8
K = 4


def passed_along(x, axis, by):
    length = lax.axis_size(axis)
    pairs = [(i, i + by) for i in range(length) if 0 <= i + by < length]
    return lax.ppermute(x, axis, pairs)


def prefix(part, axis, combine, identity):
    place = lax.axis_index(axis)
    gathered = jax.tree.map(lambda a: lax.all_gather(a, axis), part)
    state = jax.tree.map(lambda a, e: jnp.zeros_like(a) + jnp.asarray(e, a.dtype), part, identity)

    def one(lap, state):
        return combine(
            state, jax.tree.map(lambda a: lax.dynamic_index_in_dim(a, lap, 0, False), gathered)
        )

    return lax.fori_loop(0, place, one, state)


def conv_silu(values, before, taps):
    length = values.shape[0]
    padded = jnp.concatenate([before, values], 0).astype(jnp.float32)
    summed = taps[K]
    for tap_index in range(K):
        summed = summed + taps[tap_index] * padded[tap_index : tap_index + length]
    return jax.nn.silu(summed).astype(jnp.bfloat16)


def pick_group(values, group_index, axis_index):
    chosen = lax.dynamic_index_in_dim(values, group_index, axis_index, keepdims=False)
    return chosen


def body(
    tokens,
    w_zx,
    zx_scale,
    w_bc,
    bc_scale,
    w_dt,
    conv_x,
    conv_bc,
    tail_x,
    tail_bc,
    head_params,
    init_state,
    norm_gain,
):
    highest = lax.Precision.HIGHEST
    tok_rows = tokens.shape[0]
    local_heads = head_params.shape[1]
    channels = local_heads * P_SIZE
    per_group = H // G
    group_index = lax.axis_index("head") * local_heads // per_group
    bc_rows = pick_group(w_bc, group_index, 1)
    bc_scales = pick_group(bc_scale, group_index, 0)
    bc_taps = pick_group(conv_bc, group_index, 1)
    bc_tail = pick_group(tail_bc, group_index, 1)
    zx_rows = w_zx.reshape(w_zx.shape[0], 2 * channels)
    pieces = (
        lax.all_gather(zx_rows, "ctx", axis=0, tiled=True),
        lax.all_gather(bc_rows, "ctx", axis=0, tiled=True),
        lax.all_gather(w_dt, "ctx", axis=0, tiled=True),
    )
    zx_sum, bc_sum, step_sum = tuple(
        (jnp.dot(tokens, piece, preferred_element_type=jnp.float32) for piece in pieces)
    )
    zx_val = (zx_sum.reshape(tok_rows, 2, channels) * zx_scale).astype(jnp.bfloat16)
    gate = zx_val[:, 0]
    inner_in = zx_val[:, 1]
    bc_val = (bc_sum * bc_scales).astype(jnp.bfloat16)
    step_size = jax.nn.softplus(step_sum + head_params[0])
    edge = jnp.concatenate([inner_in[tok_rows - (K - 1) :], bc_val[tok_rows - (K - 1) :]], 1)
    arrived = passed_along(edge, "ctx", 1)
    previous = jnp.concatenate([tail_x, bc_tail], 1)
    arrived = jnp.where(lax.axis_index("ctx") == 0, previous, arrived)
    xconv = conv_silu(inner_in, arrived[:, :channels], conv_x)
    bconv = conv_silu(bc_val, arrived[:, channels:], bc_taps)
    b_part = bconv[:, :N]
    c_part = bconv[:, N:]
    x_heads = xconv.reshape(tok_rows, local_heads, P_SIZE).astype(jnp.float32)
    rate = -jnp.exp(head_params[1]) * step_size
    cumul = jnp.cumsum(rate, 0)
    cumul_t = cumul.T
    order = jnp.arange(tok_rows)
    lower = order[:, None] >= order[None, :]
    spread = cumul_t[:, :, None] - cumul_t[:, None, :]
    decay = jnp.where(lower[None], jnp.exp(jnp.minimum(spread, 0.0)), 0.0)
    scores = jnp.dot(c_part, b_part.T, preferred_element_type=jnp.float32)
    weights = decay * scores[None] * step_size.T[:, None, :]
    inner = jnp.einsum("hts,shp->thp", weights, x_heads, precision=highest)
    log_total = cumul[tok_rows - 1]
    fade = jnp.exp(log_total[None, :] - cumul) * step_size
    local_state = jnp.einsum(
        "sh,shp,sn->hpn", fade, x_heads, b_part.astype(jnp.float32), precision=highest
    )

    def combine(earlier, later):
        return (earlier[0] + later[0], jnp.exp(later[0])[:, None, None] * earlier[1] + later[1])

    before_log, before_state = prefix(
        (log_total, local_state),
        "ctx",
        combine,
        (jnp.zeros_like(log_total), jnp.zeros_like(local_state)),
    )
    incoming = jnp.exp(before_log)[:, None, None] * init_state + before_state
    carried = (
        jnp.einsum("tn,hpn->thp", c_part.astype(jnp.float32), incoming, precision=highest)
        * jnp.exp(cumul)[:, :, None]
    )
    y_val = inner + carried + head_params[2][None, :, None] * x_heads
    gated = y_val.reshape(tok_rows, channels) * jax.nn.silu(gate.astype(jnp.float32))
    squares = jnp.sum(gated * gated, axis=1)
    slot_hits = (jnp.arange(G) == group_index).astype(jnp.float32)
    placed = slot_hits[:, None] * squares[None, :]
    group_sums = lax.psum(placed, "head")
    totals = lax.dynamic_index_in_dim(group_sums, group_index, 0, keepdims=False)
    meansq = totals / (per_group * P_SIZE)
    mixed = gated * lax.rsqrt(meansq + 1e-05)[:, None] * norm_gain
    return mixed.astype(jnp.bfloat16)


def solution(mesh):
    return jax.shard_map(
        body,
        mesh=mesh,
        in_specs=(
            P("ctx", None),
            P("ctx", None, "head"),
            P(None, "head"),
            P("ctx", None, None),
            P(),
            P("ctx", "head"),
            P(None, "head"),
            P(),
            P(None, "head"),
            P(),
            P(None, "head"),
            P("head", None, None),
            P("head"),
        ),
        out_specs=P("ctx", "head"),
        check_vma=False,
    )
```

profile of v0, /device:TPU:30, one launch (start us, length us, event | category | flops | bytes accessed | tf_op | source)
XLA Modules:
  0.0 391.0 jit_solution(2558766528780283261)
XLA Ops:
  6.5 3.3 constant_dynamic-slice_fusion.8
  9.8 0.9 copy.38
  10.7 0.0 all-gather.9.cloned.1.call-update
  10.8 0.0 all-gather.7.cloned.1.call-start
  10.8 2.5 copy.40
  13.4 0.0 all-gather.7.cloned.1.call-update
  13.4 0.0 all-gather.11.cloned.1.call-start
  13.5 21.8 %all_gather.20 = bf16[8192,8]{0,1:T(8,128)(2,1)S(1)} all-gather(bf16[512,8]{0,1:T(8,128)(2,1)} %param.20), channel_id=1, replica_groups=mesh['ctx'=16,'head'=16] {'ctx'}, dimensions={0}, use_global_device_ids=true | all-gather | bytes 139264 | tf_op jit(solution)/shard_map/all_gather | solution.py:75
  35.3 0.8 slice_bitcast_fusion.2
  36.1 5.7 %convolution_add_fusion = f32[512,8]{0,1:T(8,128)S(1)} fusion(bf16[512,8192]{1,0:T(8,128)(2,1)} %param.15, bf16[8192,8]{0,1:T(8,128)(2,1)S(1)} %all_gather.20, f32[8]{0:T(128)S(1)} %get-tuple-element.93), kind=kOutput, calls=%fused_computation.30 | convolution fusion | flops 67112960 | bytes 8536096 | tf_op jit(solution)/shard_map/dot_general | solution.py:78
  41.8 0.1 multiply_bitcast_fusion
  41.9 1.1 reduce-window.6
  43.0 0.2 slice_reduce_fusion
  43.2 0.7 constant_dynamic-slice_fusion.7
  44.0 0.1 fusion.66
  44.0 0.2 slice_reduce_fusion.1
  44.2 0.8 constant_dynamic-slice_fusion.4
  45.0 0.1 fusion.57
  45.1 42.5 %all-gather.9.cloned.1.call-done = bf16[8192,1,512]{2,0,1:T(8,128)(2,1)} async-done(((bf16[512,1,512]{2,0,1:T(8,128)(2,1)}), bf16[8192,1,512]{2,0,1:T(8,128)(2,1)}) %all-gather.9.cloned.1.call-update) | async-done | bytes 8388624 | tf_op jit(solution)/shard_map/all_gather | solution.py:74
  87.6 10.2 %fusion.27 = bf16[512,512]{1,0:T(8,128)(2,1)S(1)} fusion(bf16[512,8192]{1,0:T(8,128)(2,1)} %param.15, bf16[8192,1,512]{2,0,1:T(8,128)(2,1)} %all-gather.9.cloned.1.call-done, f32[512]{0:T(512)S(1)} %bitcast.142), kind=kOutput, calls=%fused_computation.29 | convolution fusion | flops 4295491584 | bytes 17303552 | tf_op jit(solution)/shard_map/dot_general | solution.py:78
  97.9 0.0 copy-start.4
  97.9 0.8 copy-done.4
  98.7 107.3 %all-gather.7.cloned.1.call-done = bf16[8192,1024]{1,0:T(8,128)(2,1)} async-done(((bf16[512,1024]{1,0:T(8,128)(2,1)}), bf16[8192,1024]{1,0:T(8,128)(2,1)}) %all-gather.7.cloned.1.call-update) | async-done | bytes 16777232 | tf_op jit(solution)/shard_map/all_gather | solution.py:73
  206.0 14.3 %fusion.69 = f32[512,1024]{1,0:T(8,128)S(1)} fusion(bf16[512,8192]{1,0:T(8,128)(2,1)} %param.15, bf16[8192,1024]{1,0:T(8,128)(2,1)} %all-gather.7.cloned.1.call-done), kind=kOutput, calls=%fused_computation.115 | convolution fusion | flops 8589934592 | bytes 27262976 | tf_op jit(solution)/shard_map/dot_general | solution.py:78
  220.4 0.3 fusion.15
  220.7 1.5 collective-permute-start
  222.2 0.2 slice_convert_fusion
  222.4 3.9 collective-permute-done
  226.3 0.2 maximum_convert_fusion
  226.5 1.5 multiply_convert_fusion.1
  228.0 2.1 copy.31
  230.0 0.7 multiply_convert_fusion
  230.7 0.8 copy-done.1
  231.5 2.5 fusion.30
  234.0 0.0 all-gather.11.cloned.1.call-update
  234.0 21.3 %all-gather.2 = f32[16,1,8]{2,1,0:T(1,128)S(1)} all-gather(f32[1,1,8]{2,1,0:T(1,128)S(1)} %bitcast.141), channel_id=1, replica_groups=mesh['ctx'=16,'head'=16] {'ctx'}, dimensions={0}, use_global_device_ids=true | all-gather | bytes 544 | tf_op jit(solution)/shard_map/all_gather | solution.py:21
  255.3 0.1 iota_compare_fusion
  255.4 0.1 add_bitcast_fusion.1
  255.5 1.4 copy.35
  256.9 1.4 fusion.53
  258.2 8.7 %fusion.16 = f32[512,8,64]{0,2,1:T(8,128)} fusion(bf16[512,8,64]{0,2,1:T(8,128)(2,1)} %bitcast.122, f32[8,512]{1,0:T(8,128)S(1)} %get-tuple-element.83, f32[512,512]{1,0:T(8,128)S(1)} %fusion.53, f32[8,512]{1,0:T(8,128)S(1)} %add_bitcast_fusion.1, pred[512,512]{1,0:T(8,128)(4,1)S(1)} %iota_compare_fusion), kind=kOutput, calls=%fused_computation.21 | convolution fusion | flops 1621098496 | bytes 2916352 | tf_op jit(solution)/shard_map/hts,shp->thp/dot_general | solution.py:103
  266.9 44.0 %all-gather.11.cloned.1.call-done = f32[128,64,256]{2,1,0:T(8,128)} async-done(((f32[8,64,256]{2,1,0:T(8,128)}), f32[128,64,256]{2,1,0:T(8,128)}) %all-gather.11.cloned.1.call-update) | async-done | bytes 8388624 | tf_op jit(solution)/shard_map/all_gather | solution.py:21
  311.0 0.0 copy-start.9
  311.0 18.8 %while.12 = (s32[]{:T(128)}, f32[8]{0:T(128)S(1)}, f32[8,64,256]{2,1,0:T(8,128)S(1)}, s32[]{:T(128)}, f32[16,8]{1,0:T(8,128)S(1)}, /*index=5*/f32[16,8,64,256]{3,2,1,0:T(8,128)}, s32[]{:T(128)}, s32[]{:T(128)}, s32[]{:T(128)}) while((s32[]{:T(128)}, f32[8]{0:T(128)S(1)}, f32[8,64,256]{2,1,0:T(8,128)S(1)}, s32[]{:T(128)}, ...), condition=%wide.region_3.4_spmd, body=%wide.region_2.3_spmd.sunk | while | flops 262157 | bytes 1573167 | solution.py:29
  311.1 1.2 bitcast_add_fusion.3
  312.3 1.2 bitcast_add_fusion.3
  313.6 1.2 bitcast_add_fusion.3
  314.8 1.2 bitcast_add_fusion.3
  316.1 1.2 bitcast_add_fusion.3
  317.3 1.2 bitcast_add_fusion.3
  318.6 1.2 bitcast_add_fusion.3
  319.8 1.2 bitcast_add_fusion.3
  321.1 1.2 bitcast_add_fusion.3
  322.3 1.2 bitcast_add_fusion.3
  323.6 1.2 bitcast_add_fusion.3
  324.9 1.2 bitcast_add_fusion.3
  326.1 1.2 bitcast_add_fusion.3
  327.4 1.2 bitcast_add_fusion.3
  328.6 1.2 bitcast_add_fusion.3
  329.9 3.6 multiply_reduce_fusion
  333.5 1.6 copy.34
  335.1 0.1 broadcast_multiply_fusion
  335.1 48.1 %psum.7 = f32[8,512]{1,0:T(8,128)S(1)} all-reduce(f32[8,512]{1,0:T(8,128)S(1)} %broadcast_multiply_fusion), channel_id=1, replica_groups=mesh['ctx'=16,'head'=16] {'head'}, use_global_device_ids=true, to_apply=%region_5.6 | all-reduce | flops 4096 | bytes 32768 | tf_op jit(solution)/shard_map/psum | solution.py:129
  383.3 1.2 fusion.45
  (47 shorter events, 0.5 us)
Async XLA Ops:
  6.5 6.9 %copy-start = (bf16[3,8,512]{2,1,0:T(8,128)(2,1)S(1)}, bf16[3,8,512]{2,1,0:T(8,128)(2,1)}, u32[]{:S(2)}) copy-start(bf16[3,8,512]{2,1,0:T(8,128)(2,1)} %param.24) | copy-start | bytes 73732
  6.5 38.5 %copy-start.6 = (f32[5,512]{1,0:T(8,128)S(1)}, f32[5,512]{1,0:T(8,128)}, u32[]{:S(2)}) copy-start(f32[5,512]{1,0:T(8,128)} %param.21) | copy-start | bytes 30724
  6.5 81.1 %all-gather.9.cloned.1.call-start = ((), (), s32[]{:S(2)}) async-start(), calls=%async_computation.1 | async-start | bytes 8912896 | tf_op jit(solution)/shard_map/all_gather | solution.py:74
  10.8 195.3 %all-gather.7.cloned.1.call-start = ((), (), s32[]{:S(2)}) async-start(), calls=%async_computation | async-start | bytes 17825792 | tf_op jit(solution)/shard_map/all_gather | solution.py:73
  13.4 297.6 %all-gather.11.cloned.1.call-start = ((), (), s32[]{:S(2)}) async-start(), calls=%async_computation.2 | async-start | bytes 8912896 | tf_op jit(solution)/shard_map/all_gather | solution.py:21
  97.9 0.8 copy-start.4
  98.7 121.7 %copy-start.7 = (f32[2,512]{1,0:T(2,128)S(1)}, f32[2,512]{1,0:T(2,128)}, u32[]{:S(2)}) copy-start(f32[2,512]{1,0:T(2,128)} %param.17) | copy-start | bytes 12292
  98.7 127.6 %copy-start.8 = (bf16[3,512]{1,0:T(4,128)(2,1)S(1)}, bf16[3,512]{1,0:T(4,128)(2,1)}, u32[]{:S(2)}) copy-start(bf16[3,512]{1,0:T(4,128)(2,1)} %param.23) | copy-start | bytes 9220
  206.0 20.2 %copy-start.5 = (bf16[512,512]{1,0:T(8,128)(2,1)S(1)}, bf16[512,512]{1,0:T(8,128)(2,1)}, u32[]{:S(2)}) copy-start(bf16[512,512]{1,0:T(8,128)(2,1)} %copy-done.4) | copy-start | bytes 1572868
  220.7 5.5 %collective-permute-start = (bf16[3,1024]{1,0:T(4,128)(2,1)S(1)}, bf16[3,1024]{1,0:T(4,128)(2,1)S(1)}, u32[]{:S(2)}, u32[]{:S(2)}) collective-permute-start(bf16[3,1024]{1,0:T(4,128)(2,1)S(1)} %pad_maximum_fusion), channel_id=1, source_target_pairs={{0,16},{16,32},{32,48},{48,64},{64,80},{80,96},{96,112},{112,128},... | collective-permute-start | bytes 18440 | tf_op jit(solution)/shard_map/ppermute | solution.py:16
  230.7 0.8 copy-start.1
  258.2 71.6 %copy-start.2 = (bf16[512,512]{1,0:T(8,128)(2,1)S(1)}, bf16[512,512]{1,0:T(8,128)(2,1)}, u32[]{:S(2)}) copy-start(bf16[512,512]{1,0:T(8,128)(2,1)} %copy-done.1) | copy-start | bytes 1572868
  258.2 71.6 %copy-start.3 = (bf16[512,512]{0,1:T(8,128)(2,1)S(1)}, bf16[512,512]{0,1:T(8,128)(2,1)}, u32[]{:S(2)}) copy-start(bf16[512,512]{0,1:T(8,128)(2,1)} %copy.31) | copy-start | bytes 1572868
  311.0 72.3 %copy-start.9 = (f32[512]{0:T(512)S(1)}, f32[512]{0:T(512)}, u32[]{:S(2)}) copy-start(f32[512]{0:T(512)} %param.27) | copy-start | bytes 6148
Sparse Core Ops, SparseCore 0:
  10.9 76.6 all-gather.8
  90.1 115.9 all-gather.6
  234.2 76.7 all-gather.10
where the time goes:
time: 392 us; the launch traced here: 391 us
  waiting for transfers between devices  198 us (51%)
  blocking collectives  91.2 us (23%)
  matrix products  46.4 us (12%)
  other arithmetic  24.9 us (6%)
  local copies, waits for them, and re-layouts  15.4 us (4%)
  between operations  13.4 us (3%)
    all_gather x1, waiting for transfers between devices, body(): lax.all_gather(zx_rows, 'ctx', axis=0, tiled=True)  107 us
    psum x1, blocking collectives, body(): group_sums = lax.psum(placed, 'head')  48.1 us
    all_gather x1, waiting for transfers between devices, prefix(): gathered = jax.tree.map(lambda a: lax.all_gather(a, axis), part)  44 us
    all_gather x1, waiting for transfers between devices, body(): lax.all_gather(bc_rows, 'ctx', axis=0, tiled=True)  42.5 us
    dot_general x3, matrix products, body(): jnp.dot(tokens, piece, preferred_element_type=jnp.float32)  30.3 us
    all_gather x1, blocking collectives, body(): lax.all_gather(w_dt, 'ctx', axis=0, tiled=True)  21.8 us
    all_gather x1, blocking collectives, prefix(): gathered = jax.tree.map(lambda a: lax.all_gather(a, axis), part)  21.3 us
    add x15, other arithmetic, combine(): jnp.exp(later[0])[:, None, None] * earlier[1] + later[1]  18.1 us
  transfers between devices with their start and end apart: 4, of which 4 were waited for; matrix products, arithmetic and copies ran while one was open for 9% of the time, Pallas kernels for 0%

commit v1 on v0

--- a/solution.py
+++ b/solution.py
@@ -8,6 +8,12 @@
 N = 256
 G = 8
 K = 4
+
+
+def _define_sizes(x_in):
+    return jnp.concatenate(
+        lax.all_to_all(jnp.stack(lax.axis_size("ctx") * [x_in]), "ctx", 0, 0), axis=0
+    )
 
 
 def passed_along(x, axis, by):
@@ -70,7 +76,7 @@
     bc_tail = pick_group(tail_bc, group_index, 1)
     zx_rows = w_zx.reshape(w_zx.shape[0], 2 * channels)
     pieces = (
-        lax.all_gather(zx_rows, "ctx", axis=0, tiled=True),
+        _define_sizes(zx_rows),
         lax.all_gather(bc_rows, "ctx", axis=0, tiled=True),
         lax.all_gather(w_dt, "ctx", axis=0, tiled=True),
     )

time: 392 us -> 599 us (1.53)
  blocking collectives: 91.2 us -> 397 us
  waiting for transfers between devices: 198 us -> 49.8 us
  local copies, waits for them, and re-layouts: 15.4 us -> 60.6 us
  starting transfers between devices: 1.56 us -> 8.77 us
    all_gather x1, blocking collectives: 21.8 us -> 330 us  [body(): lax.all_gather(w_dt, 'ctx', axis=0, tiled=True)]
    all_gather x1 -> x0, waiting for transfers between devices: 107 us -> none  [body(): lax.all_gather(zx_rows, 'ctx', axis=0, tiled=True)]
    all_gather x1, waiting for transfers between devices: 42.5 us -> 0.01 us  [body(): lax.all_gather(bc_rows, 'ctx', axis=0, tiled=True)]
    all_to_all x0 -> x1, local copies, waits for them, and re-layouts: none -> 21.7 us  [_define_sizes(): lax.all_to_all(jnp.stack(lax.axis_size('ctx') * [x_in]), 'ctx', 0, 0)]
    dot_general x0 -> x1, local copies, waits for them, and re-layouts: none -> 21.3 us  [body(): jnp.dot(tokens, piece, preferred_element_type=jnp.float32)]
    another operation x2 -> x4, local copies, waits for them, and re-layouts: 0.01 us -> 8.39 us  [the longest x2 8.38 us: _define_sizes(): jnp.stack(lax.axis_size('ctx') * [x_in])]
    all_to_all x0 -> x1, starting transfers between devices: none -> 7.22 us  [_define_sizes(): lax.all_to_all(jnp.stack(lax.axis_size('ctx') * [x_in]), 'ctx', 0, 0)]
  transfers between devices with their start and end apart: 4 -> 4, of which waited for: 4 -> 2; matrix products, arithmetic and copies ran while one was open for 9% -> 11% of each run, Pallas kernels for 0% -> 0%
where the time goes in v1:
time: 599 us; the launch traced here: 597 us
  blocking collectives  397 us (66%)
  local copies, waits for them, and re-layouts  60.6 us (10%)
  waiting for transfers between devices  49.8 us (8%)
  matrix products  43.8 us (7%)
  other arithmetic  23.1 us (4%)
  between operations  13.7 us (2%)
  starting transfers between devices  8.77 us (1%)
    all_gather x1, blocking collectives, body(): lax.all_gather(w_dt, 'ctx', axis=0, tiled=True)  330 us
    psum x1, blocking collectives, body(): group_sums = lax.psum(placed, 'head')  48.1 us
    all_gather x1, waiting for transfers between devices, prefix(): gathered = jax.tree.map(lambda a: lax.all_gather(a, axis), part)  45.9 us
    dot_general x3, matrix products, body(): jnp.dot(tokens, piece, preferred_element_type=jnp.float32)  30.8 us
    all_to_all x1, local copies, waits for them, and re-layouts, _define_sizes(): lax.all_to_all(jnp.stack(lax.axis_size('ctx') * [x_in]), 'ctx', 0, 0)  21.7 us
    dot_general x1, local copies, waits for them, and re-layouts, body(): jnp.dot(tokens, piece, preferred_element_type=jnp.float32)  21.3 us
    all_gather x1, blocking collectives, prefix(): gathered = jax.tree.map(lambda a: lax.all_gather(a, axis), part)  18.7 us
    add x15, other arithmetic, combine(): jnp.exp(later[0])[:, None, None] * earlier[1] + later[1]  18.2 us
  transfers between devices with their start and end apart: 4, of which 2 were waited for; matrix products, arithmetic and copies ran while one was open for 11% of the time, Pallas kernels for 0%

profile of v1, /device:TPU:30, one launch (start us, length us, event | category | flops | bytes accessed | tf_op | source)
XLA Modules:
  0.0 597.1 jit_solution(2945144455716168796)
XLA Ops:
  6.5 2.5 copy.45
  9.0 5.9 stack.3
  14.9 7.2 %all-to-all-start = ((bf16[16,512,1024]{1,2,0:T(8,128)(2,1)}), bf16[16,512,1024]{1,2,0:T(8,128)(2,1)}, u32[]{:S(2)}, u32[]{:S(2)}) async-start(bf16[16,512,1024]{1,2,0:T(8,128)(2,1)} %stack.3), calls=%async_computation | async-start | bytes 33554432 | tf_op jit(solution)/shard_map/all_to_all | solution.py:15
  22.2 0.0 all-gather.6.cloned.1.call-start
  22.2 3.3 constant_dynamic-slice_fusion.8
  25.5 0.9 copy.48
  26.4 0.0 all-gather.6.cloned.1.call-update
  26.4 0.0 all-gather.8.cloned.1.call-start
  26.5 0.0 copy-done
  26.6 330.0 %all_gather.16 = bf16[8192,8]{0,1:T(8,128)(2,1)S(1)} all-gather(bf16[512,8]{0,1:T(8,128)(2,1)S(1)} %copy-done.4), channel_id=1, replica_groups=mesh['ctx'=16,'head'=16] {'ctx'}, dimensions={0}, use_global_device_ids=true | all-gather | bytes 139264 | tf_op jit(solution)/shard_map/all_gather | solution.py:81
  356.6 5.6 convolution_add_fusion
  362.2 0.1 multiply_bitcast_fusion
  362.3 1.1 reduce-window.6
  363.4 0.2 slice_reduce_fusion
  363.6 0.7 constant_dynamic-slice_fusion.7
  364.4 0.1 fusion.69
  364.4 0.2 slice_reduce_fusion.1
  364.6 0.8 constant_dynamic-slice_fusion.4
  365.5 0.1 fusion.60
  365.5 0.0 all-to-all-done
  365.5 21.7 %copy.37 = bf16[16,512,1024]{2,1,0:T(8,128)(2,1)} copy(bf16[16,512,1024]{1,2,0:T(8,128)(2,1)} %all-to-all-done) | data formatting | bytes 33554432 | tf_op jit(solution)/shard_map/all_to_all | solution.py:15
  387.2 21.3 %copy.38 = bf16[1024,8192]{1,0:T(8,128)(2,1)} copy(bf16[1024,8192]{0,1:T(8,128)(2,1)} %bitcast.121) | data formatting | bytes 33554432 | tf_op jit(solution)/shard_map/dot_general | solution.py:84
  408.5 10.3 %fusion.30 = bf16[512,512]{1,0:T(8,128)(2,1)S(1)} fusion(bf16[512,8192]{1,0:T(8,128)(2,1)} %param.15, bf16[8192,1,512]{2,0,1:T(8,128)(2,1)} %all-gather.6.cloned.1.call-done, f32[512]{0:T(512)S(1)} %bitcast.144), kind=kOutput, calls=%fused_computation.30 | convolution fusion | flops 4295491584 | bytes 17303552 | tf_op jit(solution)/shard_map/dot_general | solution.py:84
  418.8 0.0 copy-start.6
  418.8 14.9 %multiply_convert_fusion = bf16[512,2,512]{2,0,1:T(8,128)(2,1)S(1)} fusion(bf16[2,512,8192]{2,1,0:T(8,128)(2,1)} %bitcast.122, bf16[512,8192]{1,0:T(8,128)(2,1)} %param.15, f32[2,512]{1,0:T(2,128)S(1)} %copy-done.9), kind=kOutput, calls=%fused_computation.21 | convolution fusion | flops 8590983168 | bytes 26218496 | tf_op jit(solution)/shard_map/dot_general | solution.py:84
  433.8 1.5 collective-permute-start
  435.3 0.2 slice_convert_fusion
  435.4 3.9 collective-permute-done
  439.4 0.2 maximum_convert_fusion
  439.6 0.7 multiply_convert_fusion.2
  440.3 0.2 copy.40
  440.5 0.7 multiply_convert_fusion.1
  441.2 1.5 fusion.33
  442.7 0.0 all-gather.8.cloned.1.call-update
  442.7 18.7 %all-gather.2 = f32[16,1,8]{2,1,0:T(1,128)S(1)} all-gather(f32[1,1,8]{2,1,0:T(1,128)S(1)} %bitcast.143), channel_id=1, replica_groups=mesh['ctx'=16,'head'=16] {'ctx'}, dimensions={0}, use_global_device_ids=true | all-gather | bytes 544 | tf_op jit(solution)/shard_map/all_gather | solution.py:27
  461.4 0.1 iota_compare_fusion
  461.5 0.1 add_bitcast_fusion.1
  461.6 1.3 copy.44
  462.9 0.3 fusion.56
  463.2 7.6 %fusion.19 = f32[512,8,64]{0,2,1:T(8,128)} fusion(bf16[512,8,64]{0,2,1:T(8,128)(2,1)S(1)} %bitcast.125, f32[8,512]{1,0:T(8,128)S(1)} %get-tuple-element.89, f32[512,512]{1,0:T(8,128)S(1)} %fusion.56, f32[8,512]{1,0:T(8,128)S(1)} %add_bitcast_fusion.1, pred[512,512]{1,0:T(8,128)(4,1)S(1)} %iota_compare_fusion), kind=kOutput, calls=%fused_computation.22 | convolution fusion | flops 1621098496 | bytes 2916352 | tf_op jit(solution)/shard_map/hts,shp->thp/dot_general | solution.py:109
  470.7 45.9 %all-gather.8.cloned.1.call-done = f32[128,64,256]{2,1,0:T(8,128)} async-done(((f32[8,64,256]{2,1,0:T(8,128)}), f32[128,64,256]{2,1,0:T(8,128)}) %all-gather.8.cloned.1.call-update) | async-done | bytes 8388624 | tf_op jit(solution)/shard_map/all_gather | solution.py:27
  516.7 0.0 copy-start.1
  516.7 0.0 copy-start.7
  516.7 18.9 %while.12 = (s32[]{:T(128)}, f32[8]{0:T(128)S(1)}, f32[8,64,256]{2,1,0:T(8,128)S(1)}, s32[]{:T(128)}, f32[16,8]{1,0:T(8,128)S(1)}, /*index=5*/f32[16,8,64,256]{3,2,1,0:T(8,128)}, s32[]{:T(128)}, s32[]{:T(128)}, s32[]{:T(128)}) while((s32[]{:T(128)}, f32[8]{0:T(128)S(1)}, f32[8,64,256]{2,1,0:T(8,128)S(1)}, s32[]{:T(128)}, ...), condition=%wide.region_3.4_spmd, body=%wide.region_2.3_spmd.sunk | while | flops 262157 | bytes 1573167 | solution.py:35
  516.7 1.3 bitcast_add_fusion.3
  518.1 1.2 bitcast_add_fusion.3
  519.3 1.2 bitcast_add_fusion.3
  520.6 1.2 bitcast_add_fusion.3
  521.8 1.2 bitcast_add_fusion.3
  523.1 1.2 bitcast_add_fusion.3
  524.3 1.2 bitcast_add_fusion.3
  525.6 1.2 bitcast_add_fusion.3
  526.8 1.2 bitcast_add_fusion.3
  528.1 1.2 bitcast_add_fusion.3
  529.4 1.2 bitcast_add_fusion.3
  530.6 1.2 bitcast_add_fusion.3
  531.9 1.2 bitcast_add_fusion.3
  533.1 1.2 bitcast_add_fusion.3
  534.4 1.2 bitcast_add_fusion.3
  535.6 3.7 multiply_reduce_fusion
  539.3 1.6 copy.43
  540.9 0.1 broadcast_multiply_fusion
  540.9 48.1 %psum.7 = f32[8,512]{1,0:T(8,128)S(1)} all-reduce(f32[8,512]{1,0:T(8,128)S(1)} %broadcast_multiply_fusion), channel_id=1, replica_groups=mesh['ctx'=16,'head'=16] {'head'}, use_global_device_ids=true, to_apply=%region_5.6 | all-reduce | flops 4096 | bytes 32768 | tf_op jit(solution)/shard_map/psum | solution.py:135
  589.1 1.2 fusion.48
  (48 shorter events, 0.5 us)
Async XLA Ops:
  6.5 20.0 %copy-start = (bf16[3,8,512]{2,1,0:T(8,128)(2,1)S(1)}, bf16[3,8,512]{2,1,0:T(8,128)(2,1)}, u32[]{:S(2)}) copy-start(bf16[3,8,512]{2,1,0:T(8,128)(2,1)} %param.24) | copy-start | bytes 73732
  14.9 11.6 %copy-start.4 = (bf16[512,8]{0,1:T(8,128)(2,1)S(1)}, bf16[512,8]{0,1:T(8,128)(2,1)}, u32[]{:S(2)}) copy-start(bf16[512,8]{0,1:T(8,128)(2,1)} %param.20) | copy-start | bytes 24580
  14.9 341.6 %copy-start.8 = (f32[3,8]{1,0:T(4,128)S(1)}, f32[3,8]{1,0:T(4,128)}, u32[]{:S(2)}) copy-start(f32[3,8]{1,0:T(4,128)} %param.25) | copy-start | bytes 292
  14.9 350.6 %all-to-all-start = ((bf16[16,512,1024]{1,2,0:T(8,128)(2,1)}), bf16[16,512,1024]{1,2,0:T(8,128)(2,1)}, u32[]{:S(2)}, u32[]{:S(2)}) async-start(bf16[16,512,1024]{1,2,0:T(8,128)(2,1)} %stack.3), calls=%async_computation | async-start | bytes 33554432 | tf_op jit(solution)/shard_map/all_to_all | solution.py:15
  22.1 343.3 %copy-start.5 = (f32[5,512]{1,0:T(8,128)S(1)}, f32[5,512]{1,0:T(8,128)}, u32[]{:S(2)}) copy-start(f32[5,512]{1,0:T(8,128)} %param.21) | copy-start | bytes 30724
  22.2 386.4 %all-gather.6.cloned.1.call-start = ((), (), s32[]{:S(2)}) async-start(), calls=%async_computation.1 | async-start | bytes 8912896 | tf_op jit(solution)/shard_map/all_gather | solution.py:80
  26.4 490.2 %all-gather.8.cloned.1.call-start = ((), (), s32[]{:S(2)}) async-start(), calls=%async_computation.2 | async-start | bytes 8912896 | tf_op jit(solution)/shard_map/all_gather | solution.py:27
  408.5 10.3 %copy-start.9 = (f32[2,512]{1,0:T(2,128)S(1)}, f32[2,512]{1,0:T(2,128)}, u32[]{:S(2)}) copy-start(f32[2,512]{1,0:T(2,128)} %param.17) | copy-start | bytes 12292
  418.8 20.5 %copy-start.6 = (bf16[3,512]{1,0:T(4,128)(2,1)S(1)}, bf16[3,512]{1,0:T(4,128)(2,1)}, u32[]{:S(2)}) copy-start(bf16[3,512]{1,0:T(4,128)(2,1)} %param.23) | copy-start | bytes 9220
  433.7 5.6 copy-start.2
  433.8 5.6 collective-permute-start
  516.7 73.6 %copy-start.1 = (bf16[3,8,512]{2,1,0:T(8,128)(2,1)S(1)}, bf16[3,8,512]{2,1,0:T(8,128)(2,1)}, u32[]{:S(2)}) copy-start(bf16[3,8,512]{2,1,0:T(8,128)(2,1)} %param.24) | copy-start | bytes 73732
  516.7 72.4 %copy-start.3 = (bf16[512,2,512]{2,0,1:T(8,128)(2,1)S(1)}, bf16[512,2,512]{2,0,1:T(8,128)(2,1)}, u32[]{:S(2)}) copy-start(bf16[512,2,512]{2,0,1:T(8,128)(2,1)} %copy-done.2) | copy-start | bytes 3145732
  516.7 72.4 %copy-start.7 = (f32[512]{0:T(512)S(1)}, f32[512]{0:T(512)}, u32[]{:S(2)}) copy-start(f32[512]{0:T(512)} %param.27) | copy-start | bytes 6148
Sparse Core Ops, SparseCore 0:
  26.6 258.4 all-gather.5
  442.8 73.7 all-gather.7
